TPU v7x, 128 devices: a whole 4x4x4 slice. The times are simulated.
128 devices in a mesh: tm: 4 (over z_hi, core), mic: 32 (over y, x, z_lo).
Axes of the slice: x: 4, y: 4, z: 4 (z_hi: 2, z_lo: 2; z = z_hi * 2 + z_lo), core: 2. Of those that a mesh axis runs over, the one named last changes fastest.
Arguments:
- samples: bfloat16 [32, 4096, 4096], P('tm', 'mic'), may hold values from -6 to 6
- bin_ids: int32 [16], replicated, may hold values from 1 to 2047
- delays: int32 [4096, 4096], P('mic'), may hold values from 0 to 1023
Outputs:
- source_map: float32 [16, 4096], P('tm', 'mic')
All inputs are finite; a program needn't handle non-finite values.
Results may differ from a plain program's by a relative error of at most 0.0013.
Values may be sent and summed in bfloat16 or wider, within the bound.
No kernel may reach another device: no remote copies, remote signals or barrier semaphores. Data moves between devices by JAX's collectives and lax.ppermute only.
A program may use at most 64 MiB of HBM per device.

v0:
```python
import math
import jax
import jax.numpy as jnp
from jax import lax
from jax.sharding import PartitionSpec as P


def dft_table(bin_ids, length):
    sample_index = jnp.arange(length, dtype=jnp.int32)
    window = 0.5 - 0.5 * jnp.cos(2.0 * jnp.pi * sample_index.astype(jnp.float32) / length)
    window_norm = jnp.sqrt(jnp.sum(window * window))
    phase_index = sample_index[:, None] * bin_ids[None, :] % length
    angles = 2.0 * jnp.pi * phase_index.astype(jnp.float32) / length
    cosine = window[:, None] * jnp.cos(angles) / window_norm
    sine_part = -window[:, None] * jnp.sin(angles) / window_norm
    return jnp.stack([cosine, sine_part], axis=-1).reshape(length, -1).astype(jnp.bfloat16)


def steer_block(received, delay_cols, bins_owned, length):
    seg_count = received.shape[0]
    mic_count = received.shape[3]
    point_count = delay_cols.shape[0]

    def per_bin(entry):
        bin_value, values = entry
        phases = 2.0 * jnp.pi * (bin_value * delay_cols % length).astype(jnp.float32) / length
        steer_rows = jnp.concatenate([jnp.cos(phases), jnp.sin(phases)], axis=0).astype(
            jnp.bfloat16
        )
        product = lax.dot_general(
            values.reshape(seg_count * 2, mic_count),
            steer_rows,
            (((1,), (1,)), ((), ())),
            preferred_element_type=jnp.float32,
        )
        product = product.reshape(seg_count, 2, 2, point_count)
        real_part = product[:, 0, 0] - product[:, 1, 1]
        imag_part = product[:, 1, 0] + product[:, 0, 1]
        return jnp.stack([real_part, imag_part], axis=0)

    return lax.map(per_bin, (bins_owned, jnp.moveaxis(received, 1, 0)))


def per_device(samples, bin_ids, delays):
    length = samples.shape[2]
    transform_rows = dft_table(bin_ids, length)
    spectra = jnp.einsum("sml,lk->skm", samples, transform_rows, preferred_element_type=jnp.float32)
    spectra = spectra.reshape(samples.shape[0], bin_ids.shape[0], 2, samples.shape[1]).astype(
        jnp.bfloat16
    )
    seg_count = spectra.shape[0]
    steered = steer_block(
        lax.all_gather(spectra, "mic", axis=3, tiled=True), delays, bin_ids, length
    )
    steered = steered / math.sqrt(delays.shape[1])
    powers = jnp.sum(steered * steered, axis=(1, 2))
    welch_sum = lax.psum_scatter(powers, "tm", scatter_dimension=0, tiled=True)
    return welch_sum / (seg_count * lax.axis_size("tm"))


def solution(mesh):
    placed = (P("tm", "mic", None), P(), P("mic", None))
    return jax.shard_map(
        per_device, mesh=mesh, in_specs=placed, out_specs=P("tm", "mic"), check_vma=False
    )
```

profile of v0, /device:TPU:1, one launch (start us, length us, event | category | flops | bytes accessed | tf_op | source)
XLA Modules:
  0.0 343.3 jit_solution(9585885661330164719)
XLA Ops:
  8.0 1.9 divide_convert_fusion.1
  10.4 6.1 %convolution_convert_fusion = bf16[32,8,128]{2,0,1:T(8,128)(2,1)S(1)} fusion(bf16[4096,32,1]{0,1,2:T(8,128)(2,1)S(1)} %reshape.233, bf16[8,128,4096]{2,1,0:T(8,128)(2,1)} %param.5), kind=kOutput, calls=%fused_computation.19 | convolution fusion | flops 268468224 | bytes 8716288 | tf_op jit(solution)/shard_map/sml,lk->skm/dot_general | solution.py:47
  18.5 110.3 %all-gather.2.cloned.1.call-done = bf16[8,16,2,4096]{3,0,2,1:T(8,128)(2,1)} async-done(((bf16[8,16,2,128]{3,0,2,1:T(8,128)(2,1)}), bf16[8,16,2,4096]{3,0,2,1:T(8,128)(2,1)}) %all-gather.2.cloned.1.call-update) | async-done | bytes 2097168 | tf_op jit(solution)/shard_map/all_gather | solution.py:53
  128.8 181.1 %while.12 = (s32[]{:T(128)}, f32[16,2,8,128]{3,2,1,0:T(8,128)S(1)}, bf16[16,8,2,4096]{3,1,2,0:T(8,128)(2,1)}, s32[16]{0:T(128)S(1)}, s32[128,4096]{1,0:T(8,128)S(1)}, /*index=5*/s32[]{:T(128)}) while((s32[]{:T(128)}, f32[16,2,8,128]{3,2,1,0:T(8,128)S(1)}, bf16[16,8,2,4096]{3,1,2,0:T(8,128)(2,1)}, s32[16]{0:T(128)S(1)}, ...), condition=%wide.region_2.3_spmd, body=%wide.region_1.2_spmd.sunk | while | flops 46141440 | bytes 10674777 | solution.py:41
  129.4 8.9 %cosine_convert_fusion.2 = (bf16[128,4096]{1,0:T(8,128)(2,1)S(1)}, bf16[128,4096]{1,0:T(8,128)(2,1)S(1)}) fusion(s32[128,4096]{1,0:T(8,128)S(1)} %get-tuple-element.146, s32[]{:T(128)} %bitcast.38), kind=kLoop, calls=%fused_computation.8.clone.1 | loop fusion | flops 8388608 | bytes 4194308 | tf_op jit(solution)/shard_map/convert
  138.5 1.6 fusion.27
  140.7 8.9 %cosine_convert_fusion.2 = (bf16[128,4096]{1,0:T(8,128)(2,1)S(1)}, bf16[128,4096]{1,0:T(8,128)(2,1)S(1)}) fusion(s32[128,4096]{1,0:T(8,128)S(1)} %get-tuple-element.146, s32[]{:T(128)} %bitcast.38), kind=kLoop, calls=%fused_computation.8.clone.1 | loop fusion | flops 8388608 | bytes 4194308 | tf_op jit(solution)/shard_map/convert
  149.8 1.6 fusion.27
  152.0 8.9 %cosine_convert_fusion.2 = (bf16[128,4096]{1,0:T(8,128)(2,1)S(1)}, bf16[128,4096]{1,0:T(8,128)(2,1)S(1)}) fusion(s32[128,4096]{1,0:T(8,128)S(1)} %get-tuple-element.146, s32[]{:T(128)} %bitcast.38), kind=kLoop, calls=%fused_computation.8.clone.1 | loop fusion | flops 8388608 | bytes 4194308 | tf_op jit(solution)/shard_map/convert
  163.3 8.9 %cosine_convert_fusion.2 = (bf16[128,4096]{1,0:T(8,128)(2,1)S(1)}, bf16[128,4096]{1,0:T(8,128)(2,1)S(1)}) fusion(s32[128,4096]{1,0:T(8,128)S(1)} %get-tuple-element.146, s32[]{:T(128)} %bitcast.38), kind=kLoop, calls=%fused_computation.8.clone.1 | loop fusion | flops 8388608 | bytes 4194308 | tf_op jit(solution)/shard_map/convert
  174.6 8.9 %cosine_convert_fusion.2 = (bf16[128,4096]{1,0:T(8,128)(2,1)S(1)}, bf16[128,4096]{1,0:T(8,128)(2,1)S(1)}) fusion(s32[128,4096]{1,0:T(8,128)S(1)} %get-tuple-element.146, s32[]{:T(128)} %bitcast.38), kind=kLoop, calls=%fused_computation.8.clone.1 | loop fusion | flops 8388608 | bytes 4194308 | tf_op jit(solution)/shard_map/convert
  185.9 8.9 %cosine_convert_fusion.2 = (bf16[128,4096]{1,0:T(8,128)(2,1)S(1)}, bf16[128,4096]{1,0:T(8,128)(2,1)S(1)}) fusion(s32[128,4096]{1,0:T(8,128)S(1)} %get-tuple-element.146, s32[]{:T(128)} %bitcast.38), kind=kLoop, calls=%fused_computation.8.clone.1 | loop fusion | flops 8388608 | bytes 4194308 | tf_op jit(solution)/shard_map/convert
  195.1 1.6 fusion.27
  197.3 8.9 %cosine_convert_fusion.2 = (bf16[128,4096]{1,0:T(8,128)(2,1)S(1)}, bf16[128,4096]{1,0:T(8,128)(2,1)S(1)}) fusion(s32[128,4096]{1,0:T(8,128)S(1)} %get-tuple-element.146, s32[]{:T(128)} %bitcast.38), kind=kLoop, calls=%fused_computation.8.clone.1 | loop fusion | flops 8388608 | bytes 4194308 | tf_op jit(solution)/shard_map/convert
  206.4 1.6 fusion.27
  208.6 8.9 %cosine_convert_fusion.2 = (bf16[128,4096]{1,0:T(8,128)(2,1)S(1)}, bf16[128,4096]{1,0:T(8,128)(2,1)S(1)}) fusion(s32[128,4096]{1,0:T(8,128)S(1)} %get-tuple-element.146, s32[]{:T(128)} %bitcast.38), kind=kLoop, calls=%fused_computation.8.clone.1 | loop fusion | flops 8388608 | bytes 4194308 | tf_op jit(solution)/shard_map/convert
  217.7 1.6 fusion.27
  219.9 8.9 %cosine_convert_fusion.2 = (bf16[128,4096]{1,0:T(8,128)(2,1)S(1)}, bf16[128,4096]{1,0:T(8,128)(2,1)S(1)}) fusion(s32[128,4096]{1,0:T(8,128)S(1)} %get-tuple-element.146, s32[]{:T(128)} %bitcast.38), kind=kLoop, calls=%fused_computation.8.clone.1 | loop fusion | flops 8388608 | bytes 4194308 | tf_op jit(solution)/shard_map/convert
  229.0 1.6 fusion.27
  231.2 8.9 %cosine_convert_fusion.2 = (bf16[128,4096]{1,0:T(8,128)(2,1)S(1)}, bf16[128,4096]{1,0:T(8,128)(2,1)S(1)}) fusion(s32[128,4096]{1,0:T(8,128)S(1)} %get-tuple-element.146, s32[]{:T(128)} %bitcast.38), kind=kLoop, calls=%fused_computation.8.clone.1 | loop fusion | flops 8388608 | bytes 4194308 | tf_op jit(solution)/shard_map/convert
  240.4 1.6 fusion.27
  242.5 8.9 %cosine_convert_fusion.2 = (bf16[128,4096]{1,0:T(8,128)(2,1)S(1)}, bf16[128,4096]{1,0:T(8,128)(2,1)S(1)}) fusion(s32[128,4096]{1,0:T(8,128)S(1)} %get-tuple-element.146, s32[]{:T(128)} %bitcast.38), kind=kLoop, calls=%fused_computation.8.clone.1 | loop fusion | flops 8388608 | bytes 4194308 | tf_op jit(solution)/shard_map/convert
  251.7 1.6 fusion.27
  253.8 8.9 %cosine_convert_fusion.2 = (bf16[128,4096]{1,0:T(8,128)(2,1)S(1)}, bf16[128,4096]{1,0:T(8,128)(2,1)S(1)}) fusion(s32[128,4096]{1,0:T(8,128)S(1)} %get-tuple-element.146, s32[]{:T(128)} %bitcast.38), kind=kLoop, calls=%fused_computation.8.clone.1 | loop fusion | flops 8388608 | bytes 4194308 | tf_op jit(solution)/shard_map/convert
  263.0 1.6 fusion.27
  265.2 8.9 %cosine_convert_fusion.2 = (bf16[128,4096]{1,0:T(8,128)(2,1)S(1)}, bf16[128,4096]{1,0:T(8,128)(2,1)S(1)}) fusion(s32[128,4096]{1,0:T(8,128)S(1)} %get-tuple-element.146, s32[]{:T(128)} %bitcast.38), kind=kLoop, calls=%fused_computation.8.clone.1 | loop fusion | flops 8388608 | bytes 4194308 | tf_op jit(solution)/shard_map/convert
  276.5 8.9 %cosine_convert_fusion.2 = (bf16[128,4096]{1,0:T(8,128)(2,1)S(1)}, bf16[128,4096]{1,0:T(8,128)(2,1)S(1)}) fusion(s32[128,4096]{1,0:T(8,128)S(1)} %get-tuple-element.146, s32[]{:T(128)} %bitcast.38), kind=kLoop, calls=%fused_computation.8.clone.1 | loop fusion | flops 8388608 | bytes 4194308 | tf_op jit(solution)/shard_map/convert
  287.8 8.9 %cosine_convert_fusion.2 = (bf16[128,4096]{1,0:T(8,128)(2,1)S(1)}, bf16[128,4096]{1,0:T(8,128)(2,1)S(1)}) fusion(s32[128,4096]{1,0:T(8,128)S(1)} %get-tuple-element.146, s32[]{:T(128)} %bitcast.38), kind=kLoop, calls=%fused_computation.8.clone.1 | loop fusion | flops 8388608 | bytes 4194308 | tf_op jit(solution)/shard_map/convert
  296.9 1.6 fusion.27
  299.1 8.9 %cosine_convert_fusion.2 = (bf16[128,4096]{1,0:T(8,128)(2,1)S(1)}, bf16[128,4096]{1,0:T(8,128)(2,1)S(1)}) fusion(s32[128,4096]{1,0:T(8,128)S(1)} %get-tuple-element.146, s32[]{:T(128)} %bitcast.38), kind=kLoop, calls=%fused_computation.8.clone.1 | loop fusion | flops 8388608 | bytes 4194308 | tf_op jit(solution)/shard_map/convert
  308.3 1.6 fusion.27
  309.9 26.0 %all-reduce = f32[16,128]{1,0:T(8,128)S(1)} all-reduce(f32[16,128]{1,0:T(8,128)S(1)} %multiply_reduce_fusion), channel_id=2, replica_groups=mesh['tm'=4,'mic'=32] {'tm'}, use_global_device_ids=true, to_apply=%region_4.5.clone | all-reduce | flops 2048 | bytes 16384
  (87 shorter events, 23.5 us)
Async XLA Ops:
  6.5 122.3 %all-gather.2.cloned.1.call-start = ((), (), s32[]{:S(2)}) async-start(), calls=%async_computation | async-start | bytes 2162688 | tf_op jit(solution)/shard_map/all_gather | solution.py:53
  10.3 6.8 %copy-start.2 = (u32[128]{0:T(128)S(1)}, u32[128]{0:T(128)}, u32[]{:S(2)}) copy-start(u32[128]{0:T(128)} %constant.85) | copy-start | bytes 1540
  10.3 118.5 %copy-start = (s32[128,4096]{1,0:T(8,128)S(1)}, s32[128,4096]{1,0:T(8,128)}, u32[]{:S(2)}) copy-start(s32[128,4096]{1,0:T(8,128)} %param.7) | copy-start | bytes 6291460
  10.3 118.4 %copy-start.1 = (s32[16]{0:T(128)S(1)}, s32[16]{0:T(128)}, u32[]{:S(2)}) copy-start(s32[16]{0:T(128)} %param.6) | copy-start | bytes 196
Sparse Core Ops, SparseCore 0:
  17.3 111.4 all-gather.1
where the time goes:
time: 344 us; the launch traced here: 343 us
  other arithmetic  150 us (44%)
  waiting for transfers between devices  110 us (32%)
  matrix products  31 us (9%)
  blocking collectives  26 us (8%)
  between operations  14.9 us (4%)
  local copies, waits for them, and re-layouts  10.6 us (3%)
    another operation x17, other arithmetic  145 us
    all_gather x1, waiting for transfers between devices, per_device(): lax.all_gather(spectra, 'mic', axis=3, tiled=True)  110 us
    unnamed x1, blocking collectives  26 us
    dot_general x16, matrix products, per_bin(): lax.dot_general(values.reshape(seg_count * 2, mic_count), steer_rows, (((...  24.9 us
    dynamic_slice x16, local copies, waits for them, and re-layouts, steer_block(): return lax.map(per_bin, (bins_owned, jnp.moveaxis(received, 1, 0)))  8.9 us
  transfers between devices with their start and end apart: 1, of which 1 were waited for; matrix products, arithmetic and copies ran while one was open for 0% of the time, Pallas kernels for 0%

commit v1 on v0

--- a/solution.py
+++ b/solution.py
@@ -49,9 +49,14 @@
         jnp.bfloat16
     )
     seg_count = spectra.shape[0]
-    steered = steer_block(
-        lax.all_gather(spectra, "mic", axis=3, tiled=True), delays, bin_ids, length
-    )
+
+    def links_state(u_in, named_axis="mic"):
+        kept_arr = lax.axis_size(named_axis)
+        current_arr = jnp.stack([u_in] * kept_arr, axis=0)
+        u1 = lax.all_to_all(current_arr, named_axis, 0, 0)
+        return jnp.concatenate(u1, 3)
+
+    steered = steer_block(links_state(spectra), delays, bin_ids, length)
     steered = steered / math.sqrt(delays.shape[1])
     powers = jnp.sum(steered * steered, axis=(1, 2))
     welch_sum = lax.psum_scatter(powers, "tm", scatter_dimension=0, tiled=True)

time: 344 us -> 254 us (0.74)
  waiting for transfers between devices: 110 us -> 27.3 us
  blocking collectives: 26 us -> 9.07 us
  between operations: 14.9 us -> 1.42 us
  local copies, waits for them, and re-layouts: 10.6 us -> 23.4 us
  starting transfers between devices: 0.01 us -> 9.34 us
    all_gather x1 -> x0, waiting for transfers between devices: 110 us -> none  [per_device(): lax.all_gather(spectra, 'mic', axis=3, tiled=True)]
    all_to_all x0 -> x1, waiting for transfers between devices: none -> 27.3 us  [links_state(): u1 = lax.all_to_all(current_arr, named_axis, 0, 0)]
    unnamed x1, blocking collectives: 26 us -> 9.07 us
    all_to_all x0 -> x1, starting transfers between devices: none -> 9.34 us  [links_state(): u1 = lax.all_to_all(current_arr, named_axis, 0, 0)]
    reshape x0 -> x2, local copies, waits for them, and re-layouts: none -> 6.85 us  [links_state(): return jnp.concatenate(u1, 3)]
    while x0 -> x1, local copies, waits for them, and re-layouts: none -> 4.23 us  [steer_block(): return lax.map(per_bin, (bins_owned, jnp.moveaxis(received, 1, 0)))]
where the time goes in v1:
time: 254 us; the launch traced here: 253 us
  other arithmetic  151 us (59%)
  matrix products  30.9 us (12%)
  waiting for transfers between devices  27.3 us (11%)
  local copies, waits for them, and re-layouts  23.4 us (9%)
  starting transfers between devices  9.34 us (4%)
  blocking collectives  9.07 us (4%)
    another operation x17, other arithmetic  146 us
    all_to_all x1, waiting for transfers between devices, links_state(): u1 = lax.all_to_all(current_arr, named_axis, 0, 0)  27.3 us
    dot_general x16, matrix products, per_bin(): lax.dot_general(values.reshape(seg_count * 2, mic_count), steer_rows, (((...  24.9 us
    dynamic_slice x16, local copies, waits for them, and re-layouts, steer_block(): return lax.map(per_bin, (bins_owned, jnp.moveaxis(received, 1, 0)))  9.5 us
    all_to_all x1, starting transfers between devices, links_state(): u1 = lax.all_to_all(current_arr, named_axis, 0, 0)  9.34 us
    unnamed x1, blocking collectives  9.07 us
    reshape x2, local copies, waits for them, and re-layouts, links_state(): return jnp.concatenate(u1, 3)  6.85 us
    dot_general x1, matrix products, per_device(): jnp.einsum('sml,lk->skm', samples, transform_rows, preferred_element_type...  5.95 us
  transfers between devices with their start and end apart: 1, of which 1 were waited for; matrix products, arithmetic and copies ran while one was open for 0% of the time, Pallas kernels for 0%

profile of v1, /device:TPU:1, one launch (start us, length us, event | category | flops | bytes accessed | tf_op | source)
XLA Modules:
  0.0 253.1 jit_solution(15147883942504400595)
XLA Ops:
  1.4 1.9 divide_convert_fusion.1
  3.8 5.9 %convolution_convert_fusion = bf16[32,8,128]{2,0,1:T(8,128)(2,1)S(1)} fusion(bf16[4096,32,1]{0,1,2:T(8,128)(2,1)S(1)} %reshape.244, bf16[8,128,4096]{2,1,0:T(8,128)(2,1)} %param.5), kind=kOutput, calls=%fused_computation.19 | convolution fusion | flops 268468224 | bytes 8716288 | tf_op jit(solution)/shard_map/sml,lk->skm/dot_general | solution.py:47
  9.8 1.8 stack.11
  11.6 9.3 %all-to-all-start = ((bf16[32,8,16,2,128]{4,1,3,2,0:T(8,128)(2,1)}), bf16[32,8,16,2,128]{4,1,3,2,0:T(8,128)(2,1)S(1)}, u32[]{:S(2)}, u32[]{:S(2)}) async-start(bf16[32,8,16,2,128]{4,1,3,2,0:T(8,128)(2,1)} %stack.11), calls=%async_computation | async-start | bytes 4194304 | tf_op jit(solution)/shard_map/all_to_all | solution.py:56
  22.2 27.3 %all-to-all-done = bf16[32,8,16,2,128]{4,1,3,2,0:T(8,128)(2,1)S(1)} async-done(((bf16[32,8,16,2,128]{4,1,3,2,0:T(8,128)(2,1)}), bf16[32,8,16,2,128]{4,1,3,2,0:T(8,128)(2,1)S(1)}, u32[]{:S(2)}, u32[]{:S(2)}) %all-to-all-start) | async-done | bytes 2097184 | tf_op jit(solution)/shard_map/all_to_all | solution.py:56
  49.5 2.7 %copy.14 = bf16[8,16,2,32,128]{4,3,1,2,0:T(8,128)(2,1)} copy(bf16[8,16,2,32,128]{4,0,2,1,3:T(8,128)(2,1)S(1)} %bitcast.46) | data formatting | bytes 4194304 | tf_op jit(solution)/shard_map/reshape | solution.py:57
  52.2 4.2 %reshape.241 = bf16[8,16,2,4096]{3,1,2,0:T(8,128)(2,1)} reshape(bf16[8,16,2,32,128]{4,3,1,2,0:T(8,128)(2,1)} %copy.14) | data formatting | bytes 4194304 | tf_op jit(solution)/shard_map/reshape | solution.py:57
  56.3 4.2 %copy.15 = bf16[16,8,2,4096]{3,1,2,0:T(8,128)(2,1)} copy(bf16[16,8,2,4096]{3,0,2,1:T(8,128)(2,1)} %bitcast.47) | data formatting | bytes 4194304 | tf_op jit(solution)/shard_map/while | solution.py:41
  60.6 182.8 %while.12 = (s32[]{:T(128)}, f32[16,2,8,128]{3,2,1,0:T(8,128)S(1)}, bf16[16,8,2,4096]{3,1,2,0:T(8,128)(2,1)}, s32[16]{0:T(128)S(1)}, s32[128,4096]{1,0:T(8,128)S(1)}, /*index=5*/s32[]{:T(128)}) while((s32[]{:T(128)}, f32[16,2,8,128]{3,2,1,0:T(8,128)S(1)}, bf16[16,8,2,4096]{3,1,2,0:T(8,128)(2,1)}, s32[16]{0:T(128)S(1)}, ...), condition=%wide.region_2.3_spmd, body=%wide.region_1.2_spmd.sunk | while | flops 46141440 | bytes 10674777 | solution.py:41
  61.1 9.0 %cosine_convert_fusion.2 = (bf16[128,4096]{1,0:T(8,128)(2,1)S(1)}, bf16[128,4096]{1,0:T(8,128)(2,1)S(1)}) fusion(s32[128,4096]{1,0:T(8,128)S(1)} %get-tuple-element.161, s32[]{:T(128)} %bitcast.43), kind=kLoop, calls=%fused_computation.8.clone.1 | loop fusion | flops 8388608 | bytes 4194308 | tf_op jit(solution)/shard_map/convert
  70.4 1.6 fusion.27
  72.6 9.0 %cosine_convert_fusion.2 = (bf16[128,4096]{1,0:T(8,128)(2,1)S(1)}, bf16[128,4096]{1,0:T(8,128)(2,1)S(1)}) fusion(s32[128,4096]{1,0:T(8,128)S(1)} %get-tuple-element.161, s32[]{:T(128)} %bitcast.43), kind=kLoop, calls=%fused_computation.8.clone.1 | loop fusion | flops 8388608 | bytes 4194308 | tf_op jit(solution)/shard_map/convert
  81.8 1.6 fusion.27
  84.0 9.0 %cosine_convert_fusion.2 = (bf16[128,4096]{1,0:T(8,128)(2,1)S(1)}, bf16[128,4096]{1,0:T(8,128)(2,1)S(1)}) fusion(s32[128,4096]{1,0:T(8,128)S(1)} %get-tuple-element.161, s32[]{:T(128)} %bitcast.43), kind=kLoop, calls=%fused_computation.8.clone.1 | loop fusion | flops 8388608 | bytes 4194308 | tf_op jit(solution)/shard_map/convert
  93.2 1.6 fusion.27
  95.4 9.0 %cosine_convert_fusion.2 = (bf16[128,4096]{1,0:T(8,128)(2,1)S(1)}, bf16[128,4096]{1,0:T(8,128)(2,1)S(1)}) fusion(s32[128,4096]{1,0:T(8,128)S(1)} %get-tuple-element.161, s32[]{:T(128)} %bitcast.43), kind=kLoop, calls=%fused_computation.8.clone.1 | loop fusion | flops 8388608 | bytes 4194308 | tf_op jit(solution)/shard_map/convert
  106.8 9.0 %cosine_convert_fusion.2 = (bf16[128,4096]{1,0:T(8,128)(2,1)S(1)}, bf16[128,4096]{1,0:T(8,128)(2,1)S(1)}) fusion(s32[128,4096]{1,0:T(8,128)S(1)} %get-tuple-element.161, s32[]{:T(128)} %bitcast.43), kind=kLoop, calls=%fused_computation.8.clone.1 | loop fusion | flops 8388608 | bytes 4194308 | tf_op jit(solution)/shard_map/convert
  116.1 1.6 fusion.27
  118.3 9.0 %cosine_convert_fusion.2 = (bf16[128,4096]{1,0:T(8,128)(2,1)S(1)}, bf16[128,4096]{1,0:T(8,128)(2,1)S(1)}) fusion(s32[128,4096]{1,0:T(8,128)S(1)} %get-tuple-element.161, s32[]{:T(128)} %bitcast.43), kind=kLoop, calls=%fused_computation.8.clone.1 | loop fusion | flops 8388608 | bytes 4194308 | tf_op jit(solution)/shard_map/convert
  127.5 1.6 fusion.27
  129.7 9.0 %cosine_convert_fusion.2 = (bf16[128,4096]{1,0:T(8,128)(2,1)S(1)}, bf16[128,4096]{1,0:T(8,128)(2,1)S(1)}) fusion(s32[128,4096]{1,0:T(8,128)S(1)} %get-tuple-element.161, s32[]{:T(128)} %bitcast.43), kind=kLoop, calls=%fused_computation.8.clone.1 | loop fusion | flops 8388608 | bytes 4194308 | tf_op jit(solution)/shard_map/convert
  138.9 1.6 fusion.27
  141.1 9.0 %cosine_convert_fusion.2 = (bf16[128,4096]{1,0:T(8,128)(2,1)S(1)}, bf16[128,4096]{1,0:T(8,128)(2,1)S(1)}) fusion(s32[128,4096]{1,0:T(8,128)S(1)} %get-tuple-element.161, s32[]{:T(128)} %bitcast.43), kind=kLoop, calls=%fused_computation.8.clone.1 | loop fusion | flops 8388608 | bytes 4194308 | tf_op jit(solution)/shard_map/convert
  152.5 9.0 %cosine_convert_fusion.2 = (bf16[128,4096]{1,0:T(8,128)(2,1)S(1)}, bf16[128,4096]{1,0:T(8,128)(2,1)S(1)}) fusion(s32[128,4096]{1,0:T(8,128)S(1)} %get-tuple-element.161, s32[]{:T(128)} %bitcast.43), kind=kLoop, calls=%fused_computation.8.clone.1 | loop fusion | flops 8388608 | bytes 4194308 | tf_op jit(solution)/shard_map/convert
  164.0 9.0 %cosine_convert_fusion.2 = (bf16[128,4096]{1,0:T(8,128)(2,1)S(1)}, bf16[128,4096]{1,0:T(8,128)(2,1)S(1)}) fusion(s32[128,4096]{1,0:T(8,128)S(1)} %get-tuple-element.161, s32[]{:T(128)} %bitcast.43), kind=kLoop, calls=%fused_computation.8.clone.1 | loop fusion | flops 8388608 | bytes 4194308 | tf_op jit(solution)/shard_map/convert
  175.4 9.0 %cosine_convert_fusion.2 = (bf16[128,4096]{1,0:T(8,128)(2,1)S(1)}, bf16[128,4096]{1,0:T(8,128)(2,1)S(1)}) fusion(s32[128,4096]{1,0:T(8,128)S(1)} %get-tuple-element.161, s32[]{:T(128)} %bitcast.43), kind=kLoop, calls=%fused_computation.8.clone.1 | loop fusion | flops 8388608 | bytes 4194308 | tf_op jit(solution)/shard_map/convert
  186.8 9.0 %cosine_convert_fusion.2 = (bf16[128,4096]{1,0:T(8,128)(2,1)S(1)}, bf16[128,4096]{1,0:T(8,128)(2,1)S(1)}) fusion(s32[128,4096]{1,0:T(8,128)S(1)} %get-tuple-element.161, s32[]{:T(128)} %bitcast.43), kind=kLoop, calls=%fused_computation.8.clone.1 | loop fusion | flops 8388608 | bytes 4194308 | tf_op jit(solution)/shard_map/convert
  198.3 9.0 %cosine_convert_fusion.2 = (bf16[128,4096]{1,0:T(8,128)(2,1)S(1)}, bf16[128,4096]{1,0:T(8,128)(2,1)S(1)}) fusion(s32[128,4096]{1,0:T(8,128)S(1)} %get-tuple-element.161, s32[]{:T(128)} %bitcast.43), kind=kLoop, calls=%fused_computation.8.clone.1 | loop fusion | flops 8388608 | bytes 4194308 | tf_op jit(solution)/shard_map/convert
  209.7 9.0 %cosine_convert_fusion.2 = (bf16[128,4096]{1,0:T(8,128)(2,1)S(1)}, bf16[128,4096]{1,0:T(8,128)(2,1)S(1)}) fusion(s32[128,4096]{1,0:T(8,128)S(1)} %get-tuple-element.161, s32[]{:T(128)} %bitcast.43), kind=kLoop, calls=%fused_computation.8.clone.1 | loop fusion | flops 8388608 | bytes 4194308 | tf_op jit(solution)/shard_map/convert
  221.1 9.0 %cosine_convert_fusion.2 = (bf16[128,4096]{1,0:T(8,128)(2,1)S(1)}, bf16[128,4096]{1,0:T(8,128)(2,1)S(1)}) fusion(s32[128,4096]{1,0:T(8,128)S(1)} %get-tuple-element.161, s32[]{:T(128)} %bitcast.43), kind=kLoop, calls=%fused_computation.8.clone.1 | loop fusion | flops 8388608 | bytes 4194308 | tf_op jit(solution)/shard_map/convert
  232.5 9.0 %cosine_convert_fusion.2 = (bf16[128,4096]{1,0:T(8,128)(2,1)S(1)}, bf16[128,4096]{1,0:T(8,128)(2,1)S(1)}) fusion(s32[128,4096]{1,0:T(8,128)S(1)} %get-tuple-element.161, s32[]{:T(128)} %bitcast.43), kind=kLoop, calls=%fused_computation.8.clone.1 | loop fusion | flops 8388608 | bytes 4194308 | tf_op jit(solution)/shard_map/convert
  243.4 9.1 %all-reduce = f32[16,128]{1,0:T(8,128)S(1)} all-reduce(f32[16,128]{1,0:T(8,128)S(1)} %multiply_reduce_fusion), channel_id=2, replica_groups=mesh['tm'=4,'mic'=32] {'tm'}, use_global_device_ids=true, to_apply=%region_4.5.clone | all-reduce | flops 2048 | bytes 16384
  (90 shorter events, 31.2 us)
Async XLA Ops:
  11.6 9.4 %copy-start.2 = (u32[128]{0:T(128)S(1)}, u32[128]{0:T(128)}, u32[]{:S(2)}) copy-start(u32[128]{0:T(128)} %constant.85) | copy-start | bytes 1540
  11.6 37.9 %all-to-all-start = ((bf16[32,8,16,2,128]{4,1,3,2,0:T(8,128)(2,1)}), bf16[32,8,16,2,128]{4,1,3,2,0:T(8,128)(2,1)S(1)}, u32[]{:S(2)}, u32[]{:S(2)}) async-start(bf16[32,8,16,2,128]{4,1,3,2,0:T(8,128)(2,1)} %stack.11), calls=%async_computation | async-start | bytes 4194304 | tf_op jit(solution)/shard_map/all_to_all | solution.py:56
  56.3 4.2 %copy-start = (s32[128,4096]{1,0:T(8,128)S(1)}, s32[128,4096]{1,0:T(8,128)}, u32[]{:S(2)}) copy-start(s32[128,4096]{1,0:T(8,128)} %param.7) | copy-start | bytes 6291460
  56.3 4.2 %copy-start.1 = (s32[16]{0:T(128)S(1)}, s32[16]{0:T(128)}, u32[]{:S(2)}) copy-start(s32[16]{0:T(128)} %param.6) | copy-start | bytes 196
